TPU v7x, 32 devices: a whole 2x2x4 slice. The times are simulated.
32 devices in a mesh: gx: 8 (over y, x, core), gy: 4 (over z).
Axes of the slice: x: 2, y: 2, z: 4, core: 2. Of those that a mesh axis runs over, the one named last changes fastest.
Arguments:
- modes: float32 [3, 64, 8192], P(None, None, ('gx', 'gy')), may hold values from -6 to 6
- weights: float32 [8192], P(('gx', 'gy')), may hold values from 0.25 to 4
Outputs:
- tensor: float32 [64, 64, 64], P('gx', 'gy')
All inputs are finite; a program needn't handle non-finite values.
Results may differ from a plain program's by a relative error of at most 0.00018.
Values sent between devices are 32-bit elements; how exact they have to be, the bound alone decides.
A program may use at most 64 MiB of HBM per device.

v0:
```python
import functools
import math

import jax
import jax.numpy as jnp
from jax import lax
from jax.experimental import pallas as pl
from jax.experimental.pallas import tpu as pltpu
from jax.sharding import PartitionSpec as P

CX = 1
CY = 2
LANES = 128
MESH = pl.DeviceIdType.MESH


def partner_of(gx):
    return gx + 1 - 2 * (gx % 2)


def split(value):
    high = value.astype(jnp.bfloat16)
    low = (value - high.astype(jnp.float32)).astype(jnp.bfloat16)
    return high, low


def kernel(
    nx, ny, modes, width, height, factor,
    x_ref, w_ref, out_ref,
    other_x, other_w, edges, halos, weighted, diffs, field2, high_h, low_h, sums, landed, line, line_in,
    near_send, near_recv, far_send, far_recv, line_send, line_recv,
):
    rows, cells = x_ref.shape
    chips = nx // 2
    devices = nx * ny
    plane = width * height
    pack = max(1, LANES // plane)
    own_i = modes // nx
    own_j = modes // ny
    gx, gy = lax.axis_index("gx"), lax.axis_index("gy")
    core, place = gx % 2, gx // 2
    mate = (partner_of(gx), gy)
    minor = 2 - chips % 2
    major = chips // minor

    def shifted(s):
        return (place // minor + s // minor) % major * minor + (place % minor + s % minor) % minor

    def mirrored(s):
        return -(s // minor) % major * minor + -(s % minor) % minor

    flat = gx * ny + gy

    def beside(step, flat_id):
        other = (flat_id + step + devices) % devices
        return other // ny, other % ny

    before, after = beside(-1, flat), beside(1, flat)

    barrier = pltpu.get_barrier_semaphore()
    greeted = [mate, before, after]
    greeted += [(shifted(s) * 2 + core, gy) for s in range(1, chips) if s < minor or s % minor == 0]
    greeted += [(gx, (gy + t) % ny) for t in range(1, ny)]
    for device in greeted:
        pl.semaphore_signal(barrier, inc=1, device_id=device, device_id_type=MESH)

    for edge, start in ((0, 0), (1, cells - plane)):
        if pack == 1:
            edges[edge] = x_ref[:, start : start + plane]
        else:
            base = start // LANES * LANES
            tile = x_ref[:, base : base + LANES]
            part = rows // pack
            lane = lax.broadcasted_iota(jnp.int32, (part, LANES), 1)
            packed = jnp.zeros((part, LANES), jnp.float32)
            for p in range(pack):
                shift = (p * plane - (start - base)) % LANES
                piece = tile[p * part : (p + 1) * part]
                piece = pltpu.roll(piece, shift, 1) if shift else piece
                packed = jnp.where(lane // plane == p, piece, packed)
            edges[edge] = packed

    lane = lax.broadcasted_iota(jnp.int32, (modes, cells), 1)
    at_x, at_y = lane % width, lane // width % height

    def rolled(value, step):
        shift = (-step) % cells
        return pltpu.roll(value, shift, 1) if shift else value

    def plane_of(slot, a):
        if pack == 1:
            tile = halos[slot, a * modes : (a + 1) * modes, :]
        else:
            tiles = []
            part = rows // pack
            narrow = lax.broadcasted_iota(jnp.int32, (8, LANES), 1)
            for r in range(a * modes, (a + 1) * modes, 8):
                p, q = r // part, r % part
                piece = halos[slot, q : q + 8, :]
                full = piece
                for m in range(1, pack):
                    full = jnp.where(narrow // plane == (p + m) % pack, pltpu.roll(piece, m * plane, 1), full)
                tiles.append(full)
            tile = jnp.concatenate(tiles, axis=0)
        return jnp.concatenate([tile] * (cells // tile.shape[1]), axis=1)

    def prepare(which, ref, weight_ref):
        columns = slice(which * cells, (which + 1) * cells)
        weight = weight_ref[...] * factor
        for a in range(3):
            value = ref[a * modes : (a + 1) * modes, :]
            for g in range(nx):
                weighted[g, a, :, columns] = value[g * own_i : (g + 1) * own_i] * weight
            high, low = split(value)
            stage, half = (which, a) if a < 2 else (2, which)
            field2[stage, :modes, half * cells : (half + 1) * cells] = high
            field2[stage, modes:, half * cells : (half + 1) * cells] = low
            up = jnp.where(at_x == width - 1, rolled(value, 1 - width), rolled(value, 1))
            down = jnp.where(at_x == 0, rolled(value, width - 1), rolled(value, -1))
            diffs[a, 0, :, columns] = (up - down) * 0.5
            turn = (height - 1) * width
            up = jnp.where(at_y == height - 1, rolled(value, -turn), rolled(value, width))
            down = jnp.where(at_y == 0, rolled(value, turn), rolled(value, -width))
            diffs[a, 1, :, columns] = (up - down) * 0.5

    def prepare_z(which, ref):
        columns = slice(which * cells, (which + 1) * cells)
        for a in range(3):
            value = ref[a * modes : (a + 1) * modes, :]
            up = jnp.where(lane >= cells - plane, plane_of(2 * which + 1, a), rolled(value, plane))
            down = jnp.where(lane < plane, plane_of(2 * which, a), rolled(value, -plane))
            diffs[a, 2, :, columns] = (up - down) * 0.5

    dims = (((1,), (1,)), ((), ()))

    def block(s, stage):
        group = shifted(s) * 2 + core
        for half in range(2):
            b, which = (half, stage) if stage < 2 else (2, half)
            for c in range(0, cells, LANES):
                near_c = slice(which * cells + c, which * cells + c + LANES)
                tiles = [diffs[a, b, :, near_c] for a in range(3)]
                scales = [weighted[group, a, :, near_c] for a in range(3)]
                for i in range(own_i):
                    value = scales[0][i : i + 1] * tiles[0]
                    for a in (1, 2):
                        value = value + scales[a][i : i + 1] * tiles[a]
                    high, low = split(value)
                    place_of = slice(i * modes, (i + 1) * modes), slice(half * cells + c, half * cells + c + LANES)
                    high_h[place_of] = high
                    low_h[place_of] = low
        main = lax.dot_general(field2[stage], high_h[...], dims, preferred_element_type=jnp.float32)
        rest = lax.dot_general(field2[stage, :modes, :], low_h[...], dims, preferred_element_type=jnp.float32)
        value = main[:modes] + (main[modes:] + rest)
        sums[s] = value if stage == 0 else sums[s] + value

    def rows_of(t):
        return pl.ds(pl.multiple_of((gy + t) % ny * own_j, own_j), own_j)

    def along_minor(s, t):
        return s % minor > 0 and (s < minor or t % 2 == 0)

    def far(s, t):
        if along_minor(s, t):
            hop, slot = s % minor, s
        else:
            hop = s // minor * minor
            slot = mirrored(hop) + s % minor
        return pltpu.make_async_remote_copy(
            src_ref=sums.at[s, rows_of(t), :], dst_ref=landed.at[slot, t],
            send_sem=far_send.at[s, t], recv_sem=far_recv.at[slot, t],
            device_id=(shifted(hop) * 2 + core, gy), device_id_type=MESH,
        )

    def far_in(s, t):
        return pltpu.make_async_remote_copy(
            src_ref=landed.at[s, t], dst_ref=landed.at[s, t],
            send_sem=far_send.at[s, t], recv_sem=far_recv.at[s, t],
            device_id=mate, device_id_type=MESH,
        )

    def along(t):
        return pltpu.make_async_remote_copy(
            src_ref=line.at[t], dst_ref=line_in.at[ny - t],
            send_sem=line_send.at[t], recv_sem=line_recv.at[ny - t],
            device_id=(gx, (gy + t) % ny), device_id_type=MESH,
        )

    def along_in(t):
        return pltpu.make_async_remote_copy(
            src_ref=line_in.at[t], dst_ref=line_in.at[t],
            send_sem=line_send.at[t], recv_sem=line_recv.at[t],
            device_id=mate, device_id_type=MESH,
        )

    def sweep(stage):
        def body(s, carry):
            block(s, stage)
            return carry

        lax.fori_loop(0, chips, body, 0)

    order = list(range(ny - 1, 0, -1)) + [0]
    prepare(0, x_ref, w_ref)
    sweep(0)
    pl.semaphore_wait(barrier, len(greeted))

    def near(index, src, dst, device):
        return pltpu.make_async_remote_copy(
            src_ref=src, dst_ref=dst, send_sem=near_send.at[index], recv_sem=near_recv.at[index],
            device_id=device, device_id_type=MESH,
        )

    copies = [
        near(0, edges.at[1], halos.at[0], after),
        near(1, edges.at[0], halos.at[1], before),
        near(2, halos.at[0], halos.at[2], mate),
        near(3, halos.at[1], halos.at[3], mate),
        near(4, w_ref, other_w, mate),
        near(5, x_ref, other_x, mate),
    ]
    for index in (0, 1, 4, 5):
        copies[index].start()

    copies[4].wait_recv()
    copies[5].wait_recv()
    prepare(1, other_x, other_w)
    sweep(1)
    for index in (0, 1):
        copies[index].wait_recv()
        copies[index + 2].start()
    prepare_z(0, x_ref)
    for index in (2, 3):
        copies[index].wait_recv()
    prepare_z(1, other_x)
    cross = [s for s in range(chips) if s % minor and s >= minor]
    inner = list(range(1, minor))
    outer = [s for s in range(minor, chips, minor)]

    def waits_for(s, t):
        if minor == 1:
            return []
        if t % 2 == 0:
            return [s + 1] if s in outer else []
        return cross if s in inner else []

    for s in cross + inner + outer:
        block(s, 2)
        for t in order:
            if not waits_for(s, t):
                far(s, t).start()
    block(0, 2)
    for t in order:
        for s in inner + outer:
            if waits_for(s, t):
                value = sums[s, rows_of(t), :]
                for source in waits_for(s, t):
                    far_in(source, t).wait_recv()
                    value = value + landed[source, t]
                sums[s, rows_of(t), :] = value
                far(s, t).start()
    for t in order:
        total = sums[0, rows_of(t), :]
        for s in inner + outer:
            far_in(s, t).wait_recv()
            total = total + landed[s, t]
        line[t] = total
        if t:
            along(t).start()
    total = line[0]
    for t in range(1, ny):
        along_in(t).wait_recv()
        total = total + line_in[t]
    for i in range(own_i):
        out_ref[i] = total[:, i * modes : (i + 1) * modes]
    for copy in copies:
        copy.wait_send()
    for s in range(1, chips):
        for t in range(ny):
            far(s, t).wait_send()
    for t in range(1, ny):
        along(t).wait_send()


def per_device(modes, weights):
    mode_count, cells = modes.shape[1:]
    nx, ny = lax.axis_size("gx"), lax.axis_size("gy")
    width, height = CX * nx, CY * ny
    plane = width * height
    factor = 1.0 / math.sqrt(cells * nx * ny)
    rows = 3 * mode_count
    own_i, own_j = mode_count // nx, mode_count // ny
    pack = max(1, LANES // plane)
    edge = (rows // pack, plane * pack)
    vmem = pl.BlockSpec(memory_space=pltpu.VMEM)
    chips = nx // 2
    near_count = 6
    return pl.pallas_call(
        functools.partial(kernel, nx, ny, mode_count, width, height, factor),
        out_shape=jax.ShapeDtypeStruct((own_i, own_j, mode_count), jnp.float32),
        in_specs=[vmem, vmem],
        out_specs=vmem,
        scratch_shapes=[
            pltpu.VMEM((rows, cells), jnp.float32),
            pltpu.VMEM((1, cells), jnp.float32),
            pltpu.VMEM((2, *edge), jnp.float32),
            pltpu.VMEM((4, *edge), jnp.float32),
            pltpu.VMEM((nx, 3, own_i, 2 * cells), jnp.float32),
            pltpu.VMEM((3, 3, mode_count, 2 * cells), jnp.float32),
            pltpu.VMEM((3, 2 * mode_count, 2 * cells), jnp.bfloat16),
            pltpu.VMEM((own_i * mode_count, 2 * cells), jnp.bfloat16),
            pltpu.VMEM((own_i * mode_count, 2 * cells), jnp.bfloat16),
            pltpu.VMEM((chips, mode_count, own_i * mode_count), jnp.float32),
            pltpu.VMEM((chips, ny, own_j, own_i * mode_count), jnp.float32),
            pltpu.VMEM((ny, own_j, own_i * mode_count), jnp.float32),
            pltpu.VMEM((ny, own_j, own_i * mode_count), jnp.float32),
            pltpu.SemaphoreType.DMA((near_count,)),
            pltpu.SemaphoreType.DMA((near_count,)),
            pltpu.SemaphoreType.DMA((chips, ny)),
            pltpu.SemaphoreType.DMA((chips, ny)),
            pltpu.SemaphoreType.DMA((ny,)),
            pltpu.SemaphoreType.DMA((ny,)),
        ],
        compiler_params=pltpu.CompilerParams(collective_id=0, has_side_effects=True),
        name="tensor",
    )(modes.reshape(rows, cells), weights.reshape(1, cells))


def solution(mesh):
    return jax.shard_map(
        per_device,
        mesh=mesh,
        in_specs=(P(None, None, ("gx", "gy")), P(("gx", "gy"))),
        out_specs=P("gx", "gy", None),
        check_vma=False,
    )
```

profile of v0, /device:TPU:0, one launch (start us, length us, event | category | flops | bytes accessed | tf_op | source)
XLA Modules:
  0.0 27.1 jit_solution(2682614202957021208)
XLA Ops:
  0.0 25.6 %tensor.1 = f32[8,16,64]{2,1,0:T(8,128)} custom-call(f32[192,256]{1,0:T(8,128)} %bitcast.2, f32[1,256]{1,0:T(1,128)} %bitcast.3), custom_call_target="tpu_custom_call" | custom-call | tf_op jit(solution)/shard_map/tensor/pallas_call | solution.py:298
  25.6 1.5 %copy.4 = f32[8,16,64]{2,1,0:T(8,128)} copy(f32[8,16,64]{2,1,0:T(8,128)} %tensor.1) | data formatting | bytes 65536
where the time goes:
time: 27.3 us; the launch traced here: 27.1 us
  Pallas kernels  25.6 us (94%)
  local copies, waits for them, and re-layouts  1.47 us (5%)
    pallas_call x1, Pallas kernels, per_device(): pl.pallas_call(functools.partial(kernel, nx, ny, mode_count, width, heigh...  25.6 us
    unnamed x1, local copies, waits for them, and re-layouts  1.47 us

commit v1 on v0

v1 whole, which is shorter than its diff:
```python
import functools
import math

import jax
import jax.numpy as jnp
from jax import lax
from jax.experimental import pallas as pl
from jax.experimental.pallas import tpu as pltpu
from jax.sharding import PartitionSpec as P

CX = 1
CY = 2
LANES = 128
ROWS = 16
UNIT = 4
MESH = pl.DeviceIdType.MESH


def partner_of(gx):
    return gx + 1 - 2 * (gx % 2)


def split(value):
    high = value.astype(jnp.bfloat16)
    low = (value - high.astype(jnp.float32)).astype(jnp.bfloat16)
    return high, low


def sizes(nx, ny, modes, cells):
    width, height = CX * nx, CY * ny
    plane = width * height
    own_i = modes // nx
    unit = UNIT if own_i % UNIT == 0 else own_i
    stages = 3 if cells > plane else 2
    return width, height, plane, max(1, LANES // plane), unit, own_i // unit, stages


def kernel(
    nx, ny, modes, factor,
    x_ref, w_ref, out_ref,
    other_x, other_w, edges, halos, weighted, diffs, field, sums, landed, line, line_in,
    near_send, near_recv, far_send, far_recv, line_send, line_recv,
):
    rows, cells = x_ref.shape
    width, height, plane, pack, unit, halves, stages = sizes(nx, ny, modes, cells)
    chips = nx // 2
    devices = nx * ny
    own_j = modes // ny
    early = stages * cells
    part = rows // pack
    gx, gy = lax.axis_index("gx"), lax.axis_index("gy")
    core, place = gx % 2, gx // 2
    mate = (partner_of(gx), gy)
    minor = 2 - chips % 2
    major = chips // minor

    def shifted(s):
        return (place // minor + s // minor) % major * minor + (place % minor + s % minor) % minor

    def beside(step, x, y):
        other = (x * ny + y + step + devices) % devices
        return other // ny, other % ny

    after = beside(1, gx, gy)
    after_mate = (partner_of(after[0]), after[1])
    before = beside(-1, gx, gy)
    before_mate = beside(-1, *mate)

    barrier = pltpu.get_barrier_semaphore()
    greeted = [mate, before, before_mate]
    greeted += [(shifted(s) * 2 + core, gy) for s in range(1, chips)]
    greeted += [(gx, (gy + t) % ny) for t in range(1, ny)]
    for device in greeted:
        pl.semaphore_signal(barrier, inc=1, device_id=device, device_id_type=MESH)

    def turned(value, step):
        span = value.shape[1]
        shift = (-step) % span
        return pltpu.roll(value, shift, 1) if shift else value

    start = cells - plane
    if pack == 1:
        edges[:rows] = x_ref[:, start:]
        edges[rows:] = jnp.broadcast_to(w_ref[:, start:], (8, plane))
    else:
        base = start // LANES * LANES
        lane = lax.broadcasted_iota(jnp.int32, (part, LANES), 1)
        packed = jnp.zeros((part, LANES), jnp.float32)
        for p in range(pack):
            piece = turned(x_ref[p * part : (p + 1) * part, base : base + LANES], start - base - p * plane)
            packed = jnp.where(lane // plane == p, piece, packed)
        edges[:part] = packed
        edges[part:] = jnp.broadcast_to(turned(w_ref[:, base : base + LANES], start - base), (8, LANES))

    def near(index, src, dst, device):
        return pltpu.make_async_remote_copy(
            src_ref=src, dst_ref=dst, send_sem=near_send.at[index], recv_sem=near_recv.at[index],
            device_id=device, device_id_type=MESH,
        )

    copies = [
        near(0, w_ref, other_w, mate),
        near(1, x_ref, other_x, mate),
        near(2, edges, halos.at[0], after),
        near(3, edges, halos.at[1], after_mate),
    ]
    pl.semaphore_wait(barrier, len(greeted))
    for index in (1, 0, 2, 3):
        copies[index].start()

    span = max(plane, LANES)
    lane = lax.broadcasted_iota(jnp.int32, (modes, span), 1)
    at_x, at_y = lane % width, lane // width % height
    whole = lax.broadcasted_iota(jnp.int32, (modes, cells), 1)

    def keep(a, value, weight, scale_at, field_at):
        size = value.shape[1]
        scaled = value * weight
        for n in range(nx * halves):
            weighted[n, a, :, scale_at : scale_at + size] = scaled[n * unit : (n + 1) * unit]
        for at in field_at:
            high, low = split(value)
            field[:modes, at : at + size] = high
            field[modes:, at : at + size] = low

    def prepare(which, ref, weight_ref):
        for a in range(3):
            for c in range(0, cells, span):
                value = ref[a * modes : (a + 1) * modes, c : c + span]
                at = which * early + c
                weight = weight_ref[:, c : c + span] * factor
                keep(a, value, weight, which * cells + c, [at + a * cells] if a < stages else [])
                up = jnp.where(at_x == width - 1, turned(value, 1 - width), turned(value, 1))
                down = jnp.where(at_x == 0, turned(value, width - 1), turned(value, -1))
                diffs[a, :, at : at + span] = (up - down) * 0.5
                turn = (height - 1) * width
                up = jnp.where(at_y == height - 1, turned(value, -turn), turned(value, width))
                down = jnp.where(at_y == 0, turned(value, turn), turned(value, -width))
                diffs[a, :, at + cells : at + cells + span] = (up - down) * 0.5
            if stages == 3:
                value = ref[a * modes : (a + 1) * modes, :]
                up = jnp.where(whole < cells - plane, turned(value, plane), 0.0)
                down = jnp.where(whole >= plane, turned(value, -plane), 0.0)
                at = which * early + 2 * cells
                diffs[a, :, at : at + cells] = (up - down) * 0.5

    def prepare_late(which, ref, weight_ref):
        at, scale_at = 2 * early + which * 2 * plane, 2 * cells + which * 2 * plane
        if pack == 1:
            for a in range(3):
                mine = slice(a * modes, (a + 1) * modes)
                own, halo = ref[mine, :plane], halos[which, mine, :]
                for value, other, weight, step in (
                    (own, halo * -0.5, weight_ref[:, :plane], 0),
                    (halo, own * 0.5, halos[which, rows : rows + 1, :], plane),
                ):
                    keep(a, value, weight * factor, scale_at + step, [at + step] if a == 2 else [])
                    diffs[a, :, at + step : at + step + plane] = other
            return
        narrow = lax.broadcasted_iota(jnp.int32, (8, LANES), 1)
        low_part = narrow < plane
        weight = jnp.where(low_part[:1], weight_ref[:, :LANES], turned(halos[which, part : part + 1, :], -plane))
        for a in range(3):
            values = []
            for r in range(0, modes, 8):
                q = a * modes + r
                own = ref[q : q + 8, :LANES]
                halo = halos[which, q % part : q % part + 8, :]
                halo = turned(halo, (q // part - 1) * plane)
                values.append(jnp.where(low_part, own, halo))
                diffs[a, r : r + 8, at : at + LANES] = turned(jnp.where(low_part, own, -halo), plane) * 0.5
            keep(a, jnp.concatenate(values, axis=0), weight * factor, scale_at, [at] if a == 2 else [])

    dims = (((1,), (1,)), ((), ()))
    first = [
        [(which * early + b * cells + c, which * cells + c) for b in range(stages) for c in range(0, cells, LANES)]
        for which in range(2)
    ]
    late = [(2 * early + c, 2 * cells + c) for c in range(0, 4 * plane, LANES)]

    def block(s, half, tiles, fresh):
        group = (shifted(s) * 2 + core) * halves + half
        highs, lows = [], []
        for i in range(unit):
            for k in range(0, modes, ROWS):
                pieces = []
                for at, scale_at in tiles:
                    scales = [
                        weighted[group, a, i : i + 1, scale_at : scale_at + LANES] for a in range(3)
                    ]
                    value = scales[0] * diffs[0, k : k + ROWS, at : at + LANES]
                    for a in (1, 2):
                        value = value + scales[a] * diffs[a, k : k + ROWS, at : at + LANES]
                    pieces.append(split(value))
                highs.append(jnp.concatenate([piece[0] for piece in pieces], axis=1))
                lows.append(jnp.concatenate([piece[1] for piece in pieces], axis=1))
        high, low = jnp.concatenate(highs, axis=0), jnp.concatenate(lows, axis=0)
        columns = slice(tiles[0][0], tiles[-1][0] + LANES)
        main = lax.dot_general(field[:, columns], high, dims, preferred_element_type=jnp.float32)
        rest = lax.dot_general(field[:modes, columns], low, dims, preferred_element_type=jnp.float32)
        value = main[:modes] + (main[modes:] + rest)
        sums[s, half] = value if fresh else sums[s, half] + value

    def far(s, half, z):
        return pltpu.make_async_remote_copy(
            src_ref=sums.at[s, half, z * own_j : (z + 1) * own_j, :], dst_ref=landed.at[s, half, z],
            send_sem=far_send.at[s, half, z], recv_sem=far_recv.at[s, half, z],
            device_id=(shifted(s) * 2 + core, gy), device_id_type=MESH,
        )

    def along(half, z):
        return pltpu.make_async_remote_copy(
            src_ref=line.at[z, half], dst_ref=line_in.at[gy, half],
            send_sem=line_send.at[z, half], recv_sem=line_recv.at[gy, half],
            device_id=(gx, z), device_id_type=MESH,
        )

    def along_in(half, z):
        return pltpu.make_async_remote_copy(
            src_ref=line_in.at[z, half], dst_ref=line_in.at[z, half],
            send_sem=line_send.at[z, half], recv_sem=line_recv.at[z, half],
            device_id=mate, device_id_type=MESH,
        )

    def sweep(count, body):
        def step(u, carry):
            body(u)
            return carry

        lax.fori_loop(0, count, step, 0)

    cross = chips - 1
    prepare(0, x_ref, w_ref)
    sweep(halves, lambda u: block(cross, u, first[0], True))
    for index in (0, 1):
        copies[index].wait_recv()
    prepare(1, other_x, other_w)
    sweep(halves, lambda u: block(cross, u, first[1], False))
    for index in (2, 3):
        copies[index].wait_recv()
    prepare_late(0, x_ref, w_ref)
    prepare_late(1, other_x, other_w)

    def send(s, half):
        for z in range(ny):
            far(s, half, z).start()

    def crossing(u):
        block(cross, u, late, False)
        send(cross, u)

    def straight(u):
        s, half = cross - 1 - u % (cross - 1), u // (cross - 1)
        block(s, half, first[0] + first[1] + late, True)
        send(s, half)

    def own(half):
        block(0, half, first[0] + first[1] + late, True)
        for z in range(ny):
            total = sums[0, half, z * own_j : (z + 1) * own_j, :]
            for s in range(cross, 0, -1):
                far(s, half, z).wait_recv()
                total = total + landed[s, half, z]
            line[z, half] = total

            @pl.when(gy != z)
            def _():
                along(half, z).start()

    sweep(halves, crossing)
    sweep(halves * (cross - 1), straight)
    sweep(halves, own)
    for half in range(halves):
        total = line[gy, half]
        for t in range(1, ny):
            z = (gy + t) % ny
            along_in(half, z).wait_recv()
            total = total + line_in[z, half]
        for i in range(unit):
            out_ref[half * unit + i] = total[:, i * modes : (i + 1) * modes]
    for copy in copies:
        copy.wait_send()
    for half in range(halves):
        for s in range(1, chips):
            for z in range(ny):
                far(s, half, z).wait_send()
        for t in range(1, ny):
            along(half, (gy + t) % ny).wait_send()


def per_device(modes, weights):
    mode_count, cells = modes.shape[1:]
    nx, ny = lax.axis_size("gx"), lax.axis_size("gy")
    _, _, plane, pack, unit, halves, stages = sizes(nx, ny, mode_count, cells)
    factor = 1.0 / math.sqrt(cells * nx * ny)
    rows = 3 * mode_count
    own_i, own_j = mode_count // nx, mode_count // ny
    edge = (rows // pack + 8, plane * pack)
    depth = 2 * stages * cells + 4 * plane
    wide = unit * mode_count
    vmem = pl.BlockSpec(memory_space=pltpu.VMEM)
    chips = nx // 2
    near_count = 4
    return pl.pallas_call(
        functools.partial(kernel, nx, ny, mode_count, factor),
        out_shape=jax.ShapeDtypeStruct((own_i, own_j, mode_count), jnp.float32),
        in_specs=[vmem, vmem],
        out_specs=vmem,
        scratch_shapes=[
            pltpu.VMEM((rows, cells), jnp.float32),
            pltpu.VMEM((1, cells), jnp.float32),
            pltpu.VMEM(edge, jnp.float32),
            pltpu.VMEM((2, *edge), jnp.float32),
            pltpu.VMEM((nx * halves, 3, unit, 2 * cells + 4 * plane), jnp.float32),
            pltpu.VMEM((3, mode_count, depth), jnp.float32),
            pltpu.VMEM((2 * mode_count, depth), jnp.bfloat16),
            pltpu.VMEM((chips, halves, mode_count, wide), jnp.float32),
            pltpu.VMEM((chips, halves, ny, own_j, wide), jnp.float32),
            pltpu.VMEM((ny, halves, own_j, wide), jnp.float32),
            pltpu.VMEM((ny, halves, own_j, wide), jnp.float32),
            pltpu.SemaphoreType.DMA((near_count,)),
            pltpu.SemaphoreType.DMA((near_count,)),
            pltpu.SemaphoreType.DMA((chips, halves, ny)),
            pltpu.SemaphoreType.DMA((chips, halves, ny)),
            pltpu.SemaphoreType.DMA((ny, halves)),
            pltpu.SemaphoreType.DMA((ny, halves)),
        ],
        compiler_params=pltpu.CompilerParams(collective_id=0, has_side_effects=True),
        name="tensor",
    )(modes.reshape(rows, cells), weights.reshape(1, cells))


def solution(mesh):
    return jax.shard_map(
        per_device,
        mesh=mesh,
        in_specs=(P(None, None, ("gx", "gy")), P(("gx", "gy"))),
        out_specs=P("gx", "gy", None),
        check_vma=False,
    )
```

time: 27.3 us -> 24.7 us (0.905)
  Pallas kernels: 25.6 us -> 23 us
    pallas_call x1, Pallas kernels: 25.6 us -> 23 us  [per_device(): pl.pallas_call(functools.partial(kernel, nx, ny, mode_count, factor), out...]
where the time goes in v1:
time: 24.7 us; the launch traced here: 24.5 us
  Pallas kernels  23 us (93%)
  local copies, waits for them, and re-layouts  1.47 us (6%)
    pallas_call x1, Pallas kernels, per_device(): pl.pallas_call(functools.partial(kernel, nx, ny, mode_count, factor), out...  23 us
    unnamed x1, local copies, waits for them, and re-layouts  1.47 us

profile of v1, /device:TPU:0, one launch (start us, length us, event | category | flops | bytes accessed | tf_op | source)
XLA Modules:
  0.0 24.5 jit_solution(7970210471299969348)
XLA Ops:
  0.0 23.0 %tensor.1 = f32[8,16,64]{2,1,0:T(8,128)} custom-call(f32[192,256]{1,0:T(8,128)} %bitcast.2, f32[1,256]{1,0:T(1,128)} %bitcast.3), custom_call_target="tpu_custom_call" | custom-call | tf_op jit(solution)/shard_map/tensor/pallas_call | solution.py:304
  23.1 1.5 %copy.4 = f32[8,16,64]{2,1,0:T(8,128)} copy(f32[8,16,64]{2,1,0:T(8,128)} %tensor.1) | data formatting | bytes 65536

commit v2 on v1

--- a/solution.py
+++ b/solution.py
@@ -13,6 +13,8 @@
 LANES = 128
 ROWS = 16
 UNIT = 4
+FILL0 = 1
+FILL = 0
 MESH = pl.DeviceIdType.MESH
 
 
@@ -37,9 +39,9 @@
 
 def kernel(
     nx, ny, modes, factor,
-    x_ref, w_ref, out_ref,
-    other_x, other_w, edges, halos, weighted, diffs, field, sums, landed, line, line_in,
-    near_send, near_recv, far_send, far_recv, line_send, line_recv,
+    x_in, w_in, out_ref,
+    x_ref, w_ref, other_x, other_w, edges, halos, weighted, diffs, field, sums, landed, line, line_in,
+    load, near_send, near_recv, far_send, far_recv, line_send, line_recv,
 ):
     rows, cells = x_ref.shape
     width, height, plane, pack, unit, halves, stages = sizes(nx, ny, modes, cells)
@@ -70,8 +72,13 @@
     greeted = [mate, before, before_mate]
     greeted += [(shifted(s) * 2 + core, gy) for s in range(1, chips)]
     greeted += [(gx, (gy + t) % ny) for t in range(1, ny)]
+    loads = [pltpu.make_async_copy(x_in, x_ref, load.at[0]), pltpu.make_async_copy(w_in, w_ref, load.at[1])]
+    for copy in loads:
+        copy.start()
     for device in greeted:
         pl.semaphore_signal(barrier, inc=1, device_id=device, device_id_type=MESH)
+    for copy in loads:
+        copy.wait()
 
     def turned(value, step):
         span = value.shape[1]
@@ -99,8 +106,8 @@
         )
 
     copies = [
-        near(0, w_ref, other_w, mate),
-        near(1, x_ref, other_x, mate),
+        near(0, w_in, other_w, mate),
+        near(1, x_in, other_x, mate),
         near(2, edges, halos.at[0], after),
         near(3, edges, halos.at[1], after_mate),
     ]
@@ -201,9 +208,17 @@
         value = main[:modes] + (main[modes:] + rest)
         sums[s, half] = value if fresh else sums[s, half] + value
 
+    def rank(k):
+        if k == ny - 1:
+            return gy
+        return jnp.where(gy == 0, ny - 1 - k, k + (k - gy + ny) // ny)
+
+    def rows_of(z):
+        return pl.ds(pl.multiple_of(z * own_j, own_j), own_j)
+
     def far(s, half, z):
         return pltpu.make_async_remote_copy(
-            src_ref=sums.at[s, half, z * own_j : (z + 1) * own_j, :], dst_ref=landed.at[s, half, z],
+            src_ref=sums.at[s, half, rows_of(z), :], dst_ref=landed.at[s, half, z],
             send_sem=far_send.at[s, half, z], recv_sem=far_recv.at[s, half, z],
             device_id=(shifted(s) * 2 + core, gy), device_id_type=MESH,
         )
@@ -229,47 +244,69 @@
 
         lax.fori_loop(0, count, step, 0)
 
-    cross = chips - 1
+    others = chips - 1
+    home = -(place // minor) % major * minor + -(place % minor) % minor
+    lead = home + others * (1 - (home + others) // chips)
+    turn_by = 1 - 2 * (lead % 2)
+
+    def target(k):
+        return (lead - 1 + turn_by * k + others * chips) % others + 1
+
+    def follower(u):
+        return target(1 + u % (others - 1)), u // (others - 1)
+
     prepare(0, x_ref, w_ref)
-    sweep(halves, lambda u: block(cross, u, first[0], True))
+    sweep(halves, lambda u: block(lead, u, first[0], True))
     for index in (0, 1):
         copies[index].wait_recv()
     prepare(1, other_x, other_w)
-    sweep(halves, lambda u: block(cross, u, first[1], False))
+    sweep(halves, lambda u: block(lead, u, first[1], False))
+    ahead = jnp.where(gy == 0, FILL0, FILL)
+    sweep(ahead, lambda u: block(*follower(u), first[0] + first[1], True))
     for index in (2, 3):
         copies[index].wait_recv()
     prepare_late(0, x_ref, w_ref)
     prepare_late(1, other_x, other_w)
 
-    def send(s, half):
-        for z in range(ny):
-            far(s, half, z).start()
-
-    def crossing(u):
-        block(cross, u, late, False)
-        send(cross, u)
-
-    def straight(u):
-        s, half = cross - 1 - u % (cross - 1), u // (cross - 1)
+    def send(s, half, places):
+        for k in places:
+            far(s, half, rank(k)).start()
+
+    def leading(u):
+        block(lead, u, late, False)
+        send(lead, u, range(1))
+
+    def finish(u):
+        s, half = follower(u)
+        block(s, half, late, False)
+        send(s, half, range(ny))
+
+    def following(u):
+        s, half = follower(u)
         block(s, half, first[0] + first[1] + late, True)
-        send(s, half)
+        send(s, half, range(ny))
 
     def own(half):
         block(0, half, first[0] + first[1] + late, True)
-        for z in range(ny):
-            total = sums[0, half, z * own_j : (z + 1) * own_j, :]
-            for s in range(cross, 0, -1):
+
+    sweep(halves, leading)
+    for k in range(1, ny):
+        for half in range(halves):
+            send(lead, half, [k])
+    sweep(ahead, finish)
+    lax.fori_loop(ahead, halves * (others - 1), lambda u, carry: (following(u), carry)[1], 0)
+    sweep(halves, own)
+    for k in range(ny):
+        z = rank(k)
+        for half in range(halves):
+            total = sums[0, half, rows_of(z), :]
+            for s in range(others, 0, -1):
                 far(s, half, z).wait_recv()
                 total = total + landed[s, half, z]
             line[z, half] = total
-
-            @pl.when(gy != z)
-            def _():
+            if k < ny - 1:
                 along(half, z).start()
 
-    sweep(halves, crossing)
-    sweep(halves * (cross - 1), straight)
-    sweep(halves, own)
     for half in range(halves):
         total = line[gy, half]
         for t in range(1, ny):
@@ -304,9 +341,11 @@
     return pl.pallas_call(
         functools.partial(kernel, nx, ny, mode_count, factor),
         out_shape=jax.ShapeDtypeStruct((own_i, own_j, mode_count), jnp.float32),
-        in_specs=[vmem, vmem],
+        in_specs=[pl.BlockSpec(memory_space=pltpu.HBM)] * 2,
         out_specs=vmem,
         scratch_shapes=[
+            pltpu.VMEM((rows, cells), jnp.float32),
+            pltpu.VMEM((1, cells), jnp.float32),
             pltpu.VMEM((rows, cells), jnp.float32),
             pltpu.VMEM((1, cells), jnp.float32),
             pltpu.VMEM(edge, jnp.float32),
@@ -318,6 +357,7 @@
             pltpu.VMEM((chips, halves, ny, own_j, wide), jnp.float32),
             pltpu.VMEM((ny, halves, own_j, wide), jnp.float32),
             pltpu.VMEM((ny, halves, own_j, wide), jnp.float32),
+            pltpu.SemaphoreType.DMA((2,)),
             pltpu.SemaphoreType.DMA((near_count,)),
             pltpu.SemaphoreType.DMA((near_count,)),
             pltpu.SemaphoreType.DMA((chips, halves, ny)),
@@ -325,9 +365,9 @@
             pltpu.SemaphoreType.DMA((ny, halves)),
             pltpu.SemaphoreType.DMA((ny, halves)),
         ],
-        compiler_params=pltpu.CompilerParams(collective_id=0, has_side_effects=True),
+        compiler_params=pltpu.CompilerParams(collective_id=0, has_side_effects=True, vmem_limit_bytes=24 << 20),
         name="tensor",
-    )(modes.reshape(rows, cells), weights.reshape(1, cells))
+    )(pltpu.with_memory_space_constraint(modes.reshape(rows, cells), pltpu.HBM), pltpu.with_memory_space_constraint(weights.reshape(1, cells), pltpu.HBM))
 
 
 def solution(mesh):

time: 24.7 us -> 20.7 us (0.84)
  the two profiles are of different devices: /device:TPU:0 before, /device:TPU:2 now
where the time goes in v2:
time: 20.7 us; the launch traced here: 20.6 us
  Pallas kernels  19.9 us (96%)
  local copies, waits for them, and re-layouts  0.63 us (3%)
    pallas_call x1, Pallas kernels, per_device(): pl.pallas_call(functools.partial(kernel, nx, ny, mode_count, factor), out...  19.9 us
    unnamed x1, local copies, waits for them, and re-layouts  0.63 us

profile of v2, /device:TPU:2, one launch (start us, length us, event | category | flops | bytes accessed | tf_op | source)
XLA Modules:
  0.0 20.6 jit_solution(9759215819056597157)
XLA Ops:
  0.0 19.9 %tensor.1 = f32[8,16,64]{2,1,0:T(8,128)S(1)} custom-call(f32[192,256]{1,0:T(8,128)} %bitcast.2, f32[1,256]{1,0:T(1,128)} %bitcast.3), custom_call_target="tpu_custom_call" | custom-call | tf_op jit(solution)/shard_map/tensor/pallas_call | solution.py:341
  19.9 0.6 %copy.4 = f32[8,16,64]{2,1,0:T(8,128)} copy(f32[8,16,64]{2,1,0:T(8,128)S(1)} %tensor.1) | data formatting | bytes 65536

commit v3 on v2

--- a/solution.py
+++ b/solution.py
@@ -14,7 +14,7 @@
 ROWS = 16
 UNIT = 4
 FILL0 = 1
-FILL = 0
+FILL = 1
 MESH = pl.DeviceIdType.MESH
 
 
@@ -130,6 +130,16 @@
             field[:modes, at : at + size] = high
             field[modes:, at : at + size] = low
 
+    def across(value, at, count, step):
+        turn = (count - 1) * step
+        if span == LANES:
+            up = jnp.take_along_axis(value, jnp.where(at == count - 1, lane - turn, lane + step), axis=1)
+            down = jnp.take_along_axis(value, jnp.where(at == 0, lane + turn, lane - step), axis=1)
+        else:
+            up = jnp.where(at == count - 1, turned(value, -turn), turned(value, step))
+            down = jnp.where(at == 0, turned(value, turn), turned(value, -step))
+        return up - down
+
     def prepare(which, ref, weight_ref):
         for a in range(3):
             for c in range(0, cells, span):
@@ -137,19 +147,14 @@
                 at = which * early + c
                 weight = weight_ref[:, c : c + span] * factor
                 keep(a, value, weight, which * cells + c, [at + a * cells] if a < stages else [])
-                up = jnp.where(at_x == width - 1, turned(value, 1 - width), turned(value, 1))
-                down = jnp.where(at_x == 0, turned(value, width - 1), turned(value, -1))
-                diffs[a, :, at : at + span] = (up - down) * 0.5
-                turn = (height - 1) * width
-                up = jnp.where(at_y == height - 1, turned(value, -turn), turned(value, width))
-                down = jnp.where(at_y == 0, turned(value, turn), turned(value, -width))
-                diffs[a, :, at + cells : at + cells + span] = (up - down) * 0.5
+                diffs[a, :, at : at + span] = across(value, at_x, width, 1)
+                diffs[a, :, at + cells : at + cells + span] = across(value, at_y, height, width)
             if stages == 3:
                 value = ref[a * modes : (a + 1) * modes, :]
                 up = jnp.where(whole < cells - plane, turned(value, plane), 0.0)
                 down = jnp.where(whole >= plane, turned(value, -plane), 0.0)
                 at = which * early + 2 * cells
-                diffs[a, :, at : at + cells] = (up - down) * 0.5
+                diffs[a, :, at : at + cells] = up - down
 
     def prepare_late(which, ref, weight_ref):
         at, scale_at = 2 * early + which * 2 * plane, 2 * cells + which * 2 * plane
@@ -158,8 +163,8 @@
                 mine = slice(a * modes, (a + 1) * modes)
                 own, halo = ref[mine, :plane], halos[which, mine, :]
                 for value, other, weight, step in (
-                    (own, halo * -0.5, weight_ref[:, :plane], 0),
-                    (halo, own * 0.5, halos[which, rows : rows + 1, :], plane),
+                    (own, -halo, weight_ref[:, :plane], 0),
+                    (halo, own, halos[which, rows : rows + 1, :], plane),
                 ):
                     keep(a, value, weight * factor, scale_at + step, [at + step] if a == 2 else [])
                     diffs[a, :, at + step : at + step + plane] = other
@@ -175,7 +180,7 @@
                 halo = halos[which, q % part : q % part + 8, :]
                 halo = turned(halo, (q // part - 1) * plane)
                 values.append(jnp.where(low_part, own, halo))
-                diffs[a, r : r + 8, at : at + LANES] = turned(jnp.where(low_part, own, -halo), plane) * 0.5
+                diffs[a, r : r + 8, at : at + LANES] = turned(jnp.where(low_part, own, -halo), plane)
             keep(a, jnp.concatenate(values, axis=0), weight * factor, scale_at, [at] if a == 2 else [])
 
     dims = (((1,), (1,)), ((), ()))
@@ -218,22 +223,22 @@
 
     def far(s, half, z):
         return pltpu.make_async_remote_copy(
-            src_ref=sums.at[s, half, rows_of(z), :], dst_ref=landed.at[s, half, z],
-            send_sem=far_send.at[s, half, z], recv_sem=far_recv.at[s, half, z],
+            src_ref=sums.at[s, half, rows_of(z), :], dst_ref=landed.at[half, z, s - 1],
+            send_sem=far_send.at[0], recv_sem=far_recv.at[half, z],
             device_id=(shifted(s) * 2 + core, gy), device_id_type=MESH,
         )
 
     def along(half, z):
+        slot = (gy - z + ny) % ny - 1
         return pltpu.make_async_remote_copy(
-            src_ref=line.at[z, half], dst_ref=line_in.at[gy, half],
-            send_sem=line_send.at[z, half], recv_sem=line_recv.at[gy, half],
+            src_ref=line.at[half, z], dst_ref=line_in.at[slot, half],
+            send_sem=line_send.at[0], recv_sem=line_recv.at[0],
             device_id=(gx, z), device_id_type=MESH,
         )
 
-    def along_in(half, z):
+    def all_of(ref, send_sem, recv_sem):
         return pltpu.make_async_remote_copy(
-            src_ref=line_in.at[z, half], dst_ref=line_in.at[z, half],
-            send_sem=line_send.at[z, half], recv_sem=line_recv.at[z, half],
+            src_ref=ref, dst_ref=ref, send_sem=send_sem, recv_sem=recv_sem,
             device_id=mate, device_id_type=MESH,
         )
 
@@ -256,11 +261,13 @@
         return target(1 + u % (others - 1)), u // (others - 1)
 
     prepare(0, x_ref, w_ref)
-    sweep(halves, lambda u: block(lead, u, first[0], True))
+    for half in range(halves):
+        block(lead, half, first[0], True)
     for index in (0, 1):
         copies[index].wait_recv()
     prepare(1, other_x, other_w)
-    sweep(halves, lambda u: block(lead, u, first[1], False))
+    for half in range(halves):
+        block(lead, half, first[1], False)
     ahead = jnp.where(gy == 0, FILL0, FILL)
     sweep(ahead, lambda u: block(*follower(u), first[0] + first[1], True))
     for index in (2, 3):
@@ -289,7 +296,8 @@
     def own(half):
         block(0, half, first[0] + first[1] + late, True)
 
-    sweep(halves, leading)
+    for half in range(halves):
+        leading(half)
     for k in range(1, ny):
         for half in range(halves):
             send(lead, half, [k])
@@ -299,37 +307,32 @@
     for k in range(ny):
         z = rank(k)
         for half in range(halves):
+            all_of(landed.at[half, z], far_send.at[0], far_recv.at[half, z]).wait_recv()
             total = sums[0, half, rows_of(z), :]
-            for s in range(others, 0, -1):
-                far(s, half, z).wait_recv()
-                total = total + landed[s, half, z]
-            line[z, half] = total
+            for s in range(others):
+                total = total + landed[half, z, s]
+            line[half, z] = total
             if k < ny - 1:
                 along(half, z).start()
-
+    for copy in copies:
+        copy.wait_send()
+    all_of(sums.at[1:], far_send.at[0], far_recv.at[0, 0]).wait_send()
+    arrived = all_of(line_in, line_send.at[0], line_recv.at[0])
+    arrived.wait_recv()
     for half in range(halves):
-        total = line[gy, half]
-        for t in range(1, ny):
-            z = (gy + t) % ny
-            along_in(half, z).wait_recv()
-            total = total + line_in[z, half]
+        total = line[half, gy]
+        for t in range(ny - 1):
+            total = total + line_in[t, half]
         for i in range(unit):
             out_ref[half * unit + i] = total[:, i * modes : (i + 1) * modes]
-    for copy in copies:
-        copy.wait_send()
-    for half in range(halves):
-        for s in range(1, chips):
-            for z in range(ny):
-                far(s, half, z).wait_send()
-        for t in range(1, ny):
-            along(half, (gy + t) % ny).wait_send()
+    arrived.wait_send()
 
 
 def per_device(modes, weights):
     mode_count, cells = modes.shape[1:]
     nx, ny = lax.axis_size("gx"), lax.axis_size("gy")
     _, _, plane, pack, unit, halves, stages = sizes(nx, ny, mode_count, cells)
-    factor = 1.0 / math.sqrt(cells * nx * ny)
+    factor = 0.5 / math.sqrt(cells * nx * ny)
     rows = 3 * mode_count
     own_i, own_j = mode_count // nx, mode_count // ny
     edge = (rows // pack + 8, plane * pack)
@@ -354,16 +357,16 @@
             pltpu.VMEM((3, mode_count, depth), jnp.float32),
             pltpu.VMEM((2 * mode_count, depth), jnp.bfloat16),
             pltpu.VMEM((chips, halves, mode_count, wide), jnp.float32),
-            pltpu.VMEM((chips, halves, ny, own_j, wide), jnp.float32),
-            pltpu.VMEM((ny, halves, own_j, wide), jnp.float32),
-            pltpu.VMEM((ny, halves, own_j, wide), jnp.float32),
+            pltpu.VMEM((halves, ny, chips - 1, own_j, wide), jnp.float32),
+            pltpu.VMEM((halves, ny, own_j, wide), jnp.float32),
+            pltpu.VMEM((ny - 1, halves, own_j, wide), jnp.float32),
             pltpu.SemaphoreType.DMA((2,)),
             pltpu.SemaphoreType.DMA((near_count,)),
             pltpu.SemaphoreType.DMA((near_count,)),
-            pltpu.SemaphoreType.DMA((chips, halves, ny)),
-            pltpu.SemaphoreType.DMA((chips, halves, ny)),
-            pltpu.SemaphoreType.DMA((ny, halves)),
-            pltpu.SemaphoreType.DMA((ny, halves)),
+            pltpu.SemaphoreType.DMA((1,)),
+            pltpu.SemaphoreType.DMA((halves, ny)),
+            pltpu.SemaphoreType.DMA((1,)),
+            pltpu.SemaphoreType.DMA((1,)),
         ],
         compiler_params=pltpu.CompilerParams(collective_id=0, has_side_effects=True, vmem_limit_bytes=24 << 20),
         name="tensor",

time: 20.7 us -> 19.9 us (0.961)
  the two profiles are of different devices: /device:TPU:2 before, /device:TPU:0 now
where the time goes in v3:
time: 19.9 us; the launch traced here: 19.7 us
  Pallas kernels  19 us (95%)
  local copies, waits for them, and re-layouts  0.63 us (3%)
    pallas_call x1, Pallas kernels, per_device(): pl.pallas_call(functools.partial(kernel, nx, ny, mode_count, factor), out...  19 us
    unnamed x1, local copies, waits for them, and re-layouts  0.63 us

profile of v3, /device:TPU:0, one launch (start us, length us, event | category | flops | bytes accessed | tf_op | source)
XLA Modules:
  0.0 19.7 jit_solution(12533023785922734777)
XLA Ops:
  0.0 19.0 %tensor.1 = f32[8,16,64]{2,1,0:T(8,128)S(1)} custom-call(f32[192,256]{1,0:T(8,128)} %bitcast.2, f32[1,256]{1,0:T(1,128)} %bitcast.3), custom_call_target="tpu_custom_call" | custom-call | tf_op jit(solution)/shard_map/tensor/pallas_call | solution.py:344
  19.0 0.6 %copy.4 = f32[8,16,64]{2,1,0:T(8,128)} copy(f32[8,16,64]{2,1,0:T(8,128)S(1)} %tensor.1) | data formatting | bytes 65536

commit v4 on v3

--- a/solution.py
+++ b/solution.py
@@ -13,7 +13,7 @@
 LANES = 128
 ROWS = 16
 UNIT = 4
-FILL0 = 1
+FILL0 = 2
 FILL = 1
 MESH = pl.DeviceIdType.MESH
 
@@ -111,9 +111,17 @@
         near(2, edges, halos.at[0], after),
         near(3, edges, halos.at[1], after_mate),
     ]
-    pl.semaphore_wait(barrier, len(greeted))
-    for index in (1, 0, 2, 3):
-        copies[index].start()
+    def enter():
+        pl.semaphore_wait(barrier, len(greeted))
+        for index in (1, 0, 2, 3):
+            copies[index].start()
+
+    early_start = 1 - (place + chips - 1) // chips * ((gy + ny - 1) // ny)
+
+    @pl.when(early_start == 0)
+    def _():
+        enter()
+
 
     span = max(plane, LANES)
     lane = lax.broadcasted_iota(jnp.int32, (modes, span), 1)
@@ -216,7 +224,7 @@
     def rank(k):
         if k == ny - 1:
             return gy
-        return jnp.where(gy == 0, ny - 1 - k, k + (k - gy + ny) // ny)
+        return k + (k - gy + ny) // ny
 
     def rows_of(z):
         return pl.ds(pl.multiple_of(z * own_j, own_j), own_j)
@@ -258,11 +266,16 @@
         return (lead - 1 + turn_by * k + others * chips) % others + 1
 
     def follower(u):
-        return target(1 + u % (others - 1)), u // (others - 1)
+        return target(1 + u // halves), u % halves
 
     prepare(0, x_ref, w_ref)
     for half in range(halves):
         block(lead, half, first[0], True)
+
+    @pl.when(early_start > 0)
+    def _():
+        enter()
+
     for index in (0, 1):
         copies[index].wait_recv()
     prepare(1, other_x, other_w)
@@ -286,23 +299,26 @@
     def finish(u):
         s, half = follower(u)
         block(s, half, late, False)
-        send(s, half, range(ny))
+        send(s, half, range(ny - 1))
 
     def following(u):
         s, half = follower(u)
         block(s, half, first[0] + first[1] + late, True)
-        send(s, half, range(ny))
+        send(s, half, range(ny - 1))
 
     def own(half):
         block(0, half, first[0] + first[1] + late, True)
 
     for half in range(halves):
-        leading(half)
-    for k in range(1, ny):
+        block(lead, half, late, False)
+    for k in range(ny - 1):
         for half in range(halves):
             send(lead, half, [k])
     sweep(ahead, finish)
     lax.fori_loop(ahead, halves * (others - 1), lambda u, carry: (following(u), carry)[1], 0)
+    for half in range(halves):
+        send(lead, half, [ny - 1])
+    sweep(halves * (others - 1), lambda u: send(*follower(u), [ny - 1]))
     sweep(halves, own)
     for k in range(ny):
         z = rank(k)

time: 19.9 us -> 19.4 us (0.975)
  Pallas kernels: 19 us -> 18.7 us
    pallas_call x1, Pallas kernels: 19 us -> 18.7 us  [per_device(): pl.pallas_call(functools.partial(kernel, nx, ny, mode_count, factor), out...]
where the time goes in v4:
time: 19.4 us; the launch traced here: 19.3 us
  Pallas kernels  18.7 us (96%)
  local copies, waits for them, and re-layouts  0.63 us (3%)
    pallas_call x1, Pallas kernels, per_device(): pl.pallas_call(functools.partial(kernel, nx, ny, mode_count, factor), out...  18.7 us
    unnamed x1, local copies, waits for them, and re-layouts  0.63 us

profile of v4, /device:TPU:0, one launch (start us, length us, event | category | flops | bytes accessed | tf_op | source)
XLA Modules:
  0.0 19.3 jit_solution(8022595028871778382)
XLA Ops:
  0.0 18.7 %tensor.1 = f32[8,16,64]{2,1,0:T(8,128)S(1)} custom-call(f32[192,256]{1,0:T(8,128)} %bitcast.2, f32[1,256]{1,0:T(1,128)} %bitcast.3), custom_call_target="tpu_custom_call" | custom-call | tf_op jit(solution)/shard_map/tensor/pallas_call | solution.py:360
  18.7 0.6 %copy.4 = f32[8,16,64]{2,1,0:T(8,128)} copy(f32[8,16,64]{2,1,0:T(8,128)S(1)} %tensor.1) | data formatting | bytes 65536

commit v5 on v4

--- a/solution.py
+++ b/solution.py
@@ -41,7 +41,7 @@
     nx, ny, modes, factor,
     x_in, w_in, out_ref,
     x_ref, w_ref, other_x, other_w, edges, halos, weighted, diffs, field, sums, landed, line, line_in,
-    load, near_send, near_recv, far_send, far_recv, line_send, line_recv,
+    joined, load, near_send, near_recv, far_send, far_recv, line_send, line_recv,
 ):
     rows, cells = x_ref.shape
     width, height, plane, pack, unit, halves, stages = sizes(nx, ny, modes, cells)
@@ -69,14 +69,26 @@
     before_mate = beside(-1, *mate)
 
     barrier = pltpu.get_barrier_semaphore()
-    greeted = [mate, before, before_mate]
-    greeted += [(shifted(s) * 2 + core, gy) for s in range(1, chips)]
-    greeted += [(gx, (gy + t) % ny) for t in range(1, ny)]
     loads = [pltpu.make_async_copy(x_in, x_ref, load.at[0]), pltpu.make_async_copy(w_in, w_ref, load.at[1])]
     for copy in loads:
         copy.start()
-    for device in greeted:
+    for device in (mate, before, before_mate):
         pl.semaphore_signal(barrier, inc=1, device_id=device, device_id_type=MESH)
+
+    def greet(semaphore, sign):
+        for q in range(chips):
+
+            @pl.when((q - place) * sign > 0)
+            def _():
+                pl.semaphore_signal(semaphore[0], inc=1, device_id=(q * 2 + core, gy), device_id_type=MESH)
+
+        for z in range(ny):
+
+            @pl.when((z - gy) * sign > 0)
+            def _():
+                pl.semaphore_signal(semaphore[1], inc=1, device_id=(gx, z), device_id_type=MESH)
+
+    greet((barrier, barrier), 1)
     for copy in loads:
         copy.wait()
 
@@ -112,11 +124,12 @@
         near(3, edges, halos.at[1], after_mate),
     ]
     def enter():
-        pl.semaphore_wait(barrier, len(greeted))
-        for index in (1, 0, 2, 3):
+        pl.semaphore_wait(barrier, 3 + place + gy)
+        for index in (2, 3, 1, 0):
             copies[index].start()
-
-    early_start = 1 - (place + chips - 1) // chips * ((gy + ny - 1) // ny)
+        greet((joined.at[0], joined.at[1]), -1)
+
+    early_start = 1 - (gy + ny - 1) // ny
 
     @pl.when(early_start == 0)
     def _():
@@ -311,6 +324,11 @@
 
     for half in range(halves):
         block(lead, half, late, False)
+
+    @pl.when(place < chips - 1)
+    def _():
+        pl.semaphore_wait(joined.at[0], chips - 1 - place)
+
     for k in range(ny - 1):
         for half in range(halves):
             send(lead, half, [k])
@@ -320,6 +338,11 @@
         send(lead, half, [ny - 1])
     sweep(halves * (others - 1), lambda u: send(*follower(u), [ny - 1]))
     sweep(halves, own)
+
+    @pl.when(gy < ny - 1)
+    def _():
+        pl.semaphore_wait(joined.at[1], ny - 1 - gy)
+
     for k in range(ny):
         z = rank(k)
         for half in range(halves):
@@ -376,6 +399,7 @@
             pltpu.VMEM((halves, ny, chips - 1, own_j, wide), jnp.float32),
             pltpu.VMEM((halves, ny, own_j, wide), jnp.float32),
             pltpu.VMEM((ny - 1, halves, own_j, wide), jnp.float32),
+            pltpu.SemaphoreType.REGULAR((2,)),
             pltpu.SemaphoreType.DMA((2,)),
             pltpu.SemaphoreType.DMA((near_count,)),
             pltpu.SemaphoreType.DMA((near_count,)),

time: 19.4 us -> 19.2 us (0.990)
  Pallas kernels: 18.7 us -> 18.5 us
    pallas_call x1, Pallas kernels: 18.7 us -> 18.5 us  [per_device(): pl.pallas_call(functools.partial(kernel, nx, ny, mode_count, factor), out...]
where the time goes in v5:
time: 19.2 us; the launch traced here: 19.1 us
  Pallas kernels  18.5 us (96%)
  local copies, waits for them, and re-layouts  0.63 us (3%)
    pallas_call x1, Pallas kernels, per_device(): pl.pallas_call(functools.partial(kernel, nx, ny, mode_count, factor), out...  18.5 us
    unnamed x1, local copies, waits for them, and re-layouts  0.63 us

profile of v5, /device:TPU:0, one launch (start us, length us, event | category | flops | bytes accessed | tf_op | source)
XLA Modules:
  0.0 19.1 jit_solution(10574740013253363710)
XLA Ops:
  0.0 18.5 %tensor.1 = f32[8,16,64]{2,1,0:T(8,128)S(1)} custom-call(f32[192,256]{1,0:T(8,128)} %bitcast.2, f32[1,256]{1,0:T(1,128)} %bitcast.3), custom_call_target="tpu_custom_call" | custom-call | tf_op jit(solution)/shard_map/tensor/pallas_call | solution.py:383
  18.5 0.6 %copy.4 = f32[8,16,64]{2,1,0:T(8,128)} copy(f32[8,16,64]{2,1,0:T(8,128)S(1)} %tensor.1) | data formatting | bytes 65536

commit v6 on v5

--- a/solution.py
+++ b/solution.py
@@ -296,9 +296,9 @@
         block(lead, half, first[1], False)
     ahead = jnp.where(gy == 0, FILL0, FILL)
     sweep(ahead, lambda u: block(*follower(u), first[0] + first[1], True))
-    for index in (2, 3):
-        copies[index].wait_recv()
+    copies[2].wait_recv()
     prepare_late(0, x_ref, w_ref)
+    copies[3].wait_recv()
     prepare_late(1, other_x, other_w)
 
     def send(s, half, places):
@@ -336,8 +336,8 @@
     lax.fori_loop(ahead, halves * (others - 1), lambda u, carry: (following(u), carry)[1], 0)
     for half in range(halves):
         send(lead, half, [ny - 1])
+    sweep(halves, own)
     sweep(halves * (others - 1), lambda u: send(*follower(u), [ny - 1]))
-    sweep(halves, own)
 
     @pl.when(gy < ny - 1)
     def _():

time: 19.2 us -> 19.2 us (level)
  no operation moved by 1% of the time
where the time goes in v6:
time: 19.2 us; the launch traced here: 19.1 us
  Pallas kernels  18.5 us (96%)
  local copies, waits for them, and re-layouts  0.63 us (3%)
    pallas_call x1, Pallas kernels, per_device(): pl.pallas_call(functools.partial(kernel, nx, ny, mode_count, factor), out...  18.5 us
    unnamed x1, local copies, waits for them, and re-layouts  0.63 us

profile of v6, /device:TPU:0, one launch (start us, length us, event | category | flops | bytes accessed | tf_op | source)
XLA Modules:
  0.0 19.1 jit_solution(7477420639351859127)
XLA Ops:
  0.0 18.5 %tensor.1 = f32[8,16,64]{2,1,0:T(8,128)S(1)} custom-call(f32[192,256]{1,0:T(8,128)} %bitcast.2, f32[1,256]{1,0:T(1,128)} %bitcast.3), custom_call_target="tpu_custom_call" | custom-call | tf_op jit(solution)/shard_map/tensor/pallas_call | solution.py:383
  18.5 0.6 %copy.4 = f32[8,16,64]{2,1,0:T(8,128)} copy(f32[8,16,64]{2,1,0:T(8,128)S(1)} %tensor.1) | data formatting | bytes 65536
